TPU v7x, 512 devices: a whole 4x8x8 slice. The times are simulated.
512 devices in a mesh: dp: 4 (over x), seq: 16 (over z, core), tensor: 8 (over y).
Axes of the slice: x: 4, y: 8, z: 8, core: 2. Of those that a mesh axis runs over, the one named last changes fastest.
Arguments:
- hidden: bfloat16 [8192, 8192], P(('dp', 'seq'), 'tensor'), may hold values from -6 to 6
- queries: bfloat16 [8192, 8192], P(('dp', 'seq'), 'tensor'), may hold values from -14 to 14
- kv_weight: bfloat16 [8192, 2048], P('seq', 'tensor'), may hold values from -0.0625 to 0.0625
- parents: int32 [4, 16], P('dp'), may hold values from -1 to 14, as said below
- out_grad: bfloat16 [8192, 8192], P(('dp', 'seq'), 'tensor'), may hold values from -6 to 6
Outputs:
- attended: bfloat16 [8192, 8192], P(('dp', 'seq'), 'tensor')
- query_grad: float32 [8192, 8192], P(('dp', 'seq'), 'tensor')
- weight_grad: float32 [8192, 2048], P('seq', 'tensor')
Inputs may be any that keep to these rules, and one draw needn't show every extreme that they name: parents[g, n] is -1 where node block n begins a new tree of group g (always for n = 0), else an earlier node block of the same group; the last node block of every group has parent 16 - 2.
All inputs are finite; a program needn't handle non-finite values.
Results may differ from a plain program's by a relative error of at most 0.012.
The roundings to bfloat16 on the way count: a program that leaves them out, or rounds other values in their place, can miss the bound.
Values may be sent and summed in bfloat16 or wider, within the bound.
No kernel may reach another device: no remote copies, remote signals or barrier semaphores. Data moves between devices by JAX's collectives and lax.ppermute only.
A program may use at most 64 MiB of HBM per device.

v0:
```python
import math
import jax
import jax.numpy as jnp
from jax import lax
from jax.sharding import PartitionSpec as P

HD = 128


def attend_block(query_blk, grad_blk, keys_head, values_head, visible):
    inv_root = 1.0 / math.sqrt(query_blk.shape[-1])
    scores = (
        jnp.einsum("thd,jd->htj", query_blk, keys_head, preferred_element_type=jnp.float32)
        * inv_root
    )
    scores = jnp.where(visible[None], scores, -jnp.inf)
    row_top = jnp.max(scores, axis=-1, keepdims=True)
    expons = jnp.exp(scores - row_top)
    probs_f = expons / jnp.sum(expons, axis=-1, keepdims=True)
    weights = probs_f.astype(jnp.bfloat16)
    mixed_f = jnp.einsum("htj,jd->thd", weights, values_head, preferred_element_type=jnp.float32)
    prob_grad = jnp.einsum("thd,jd->htj", grad_blk, values_head, preferred_element_type=jnp.float32)
    inner_sum = jnp.transpose(jnp.sum(grad_blk.astype(jnp.float32) * mixed_f, axis=-1), (1, 0))
    score_grad = (probs_f * (prob_grad - inner_sum[:, :, None]) * inv_root).astype(jnp.bfloat16)
    query_grad = jnp.einsum(
        "htj,jd->thd", score_grad, keys_head, preferred_element_type=jnp.float32
    )
    key_grad = jnp.einsum("htj,thd->jd", score_grad, query_blk, preferred_element_type=jnp.float32)
    value_grad = jnp.einsum("htj,thd->jd", weights, grad_blk, preferred_element_type=jnp.float32)
    return (mixed_f.astype(jnp.bfloat16), query_grad, key_grad, value_grad)


def per_device(hidden, queries, kv_weight, parents, out_grad):
    tok_rows = queries.shape[0]
    head_size = HD
    kv_local = kv_weight.shape[1] // (2 * head_size)
    heads_local = queries.shape[1] // head_size
    heads_per = heads_local // kv_local
    block_heads = max(1, min(heads_per, 512 // tok_rows))
    block_count = heads_per // block_heads
    node_count = lax.axis_size("seq")
    my_node = lax.axis_index("seq")
    group_rows = tok_rows * node_count
    whole_rows = lax.all_gather(hidden, "tensor", axis=1, tiled=True)
    traded = lax.all_to_all(whole_rows, "seq", split_axis=1, concat_axis=0, tiled=True)
    partial_kv = jnp.dot(traded, kv_weight, preferred_element_type=jnp.float32)
    kv_all = lax.psum(partial_kv, "seq").astype(jnp.bfloat16)
    parent_list = parents[0]
    node_ids = jnp.arange(node_count, dtype=jnp.int32)

    def follow(step_index, state_pair):
        current, marked = state_pair
        marked = jnp.maximum(marked, (node_ids == current).astype(jnp.int32))
        current = jnp.where(current >= 0, parent_list[jnp.maximum(current, 0)], -1)
        return (current, marked)

    start_pair = (parent_list[my_node], jnp.zeros((node_count,), jnp.int32))
    final_pair = lax.fori_loop(0, node_count, follow, start_pair)
    key_above = jnp.broadcast_to(final_pair[1][:, None] > 0, (node_count, tok_rows)).reshape(
        group_rows
    )
    key_node = jnp.arange(group_rows, dtype=jnp.int32) // tok_rows
    key_pos = jnp.arange(group_rows, dtype=jnp.int32) % tok_rows
    query_pos = jnp.arange(tok_rows, dtype=jnp.int32)
    visible = key_above[None, :] | (key_node == my_node)[None, :] & (
        key_pos[None, :] <= query_pos[:, None]
    )
    kv_heads = kv_all.reshape(group_rows, kv_local, 2, head_size).transpose(1, 0, 2, 3)
    query_split = queries.reshape(
        tok_rows, kv_local, block_count, block_heads, head_size
    ).transpose(1, 2, 0, 3, 4)
    grad_split = out_grad.reshape(
        tok_rows, kv_local, block_count, block_heads, head_size
    ).transpose(1, 2, 0, 3, 4)

    def per_head(packed):
        query_head, grad_head, head_kv = packed
        keys_head = head_kv[:, 0, :]
        values_head = head_kv[:, 1, :]

        def per_part(running, block_pair):
            mixed_blk, qgrad_blk, key_grad, value_grad = attend_block(
                block_pair[0], block_pair[1], keys_head, values_head, visible
            )
            return ((running[0] + key_grad, running[1] + value_grad), (mixed_blk, qgrad_blk))

        zero_grad = jnp.zeros((group_rows, head_size), jnp.float32)
        sums_pair, outputs = lax.scan(per_part, (zero_grad, zero_grad), (query_head, grad_head))
        return (outputs[0], outputs[1], jnp.stack([sums_pair[0], sums_pair[1]], axis=1))

    mixed_all, qgrad_all, kv_terms = lax.map(per_head, (query_split, grad_split, kv_heads))
    attended = mixed_all.transpose(2, 0, 1, 3, 4).reshape(tok_rows, heads_local * head_size)
    query_grad = qgrad_all.transpose(2, 0, 1, 3, 4).reshape(tok_rows, heads_local * head_size)
    kv_terms = kv_terms.transpose(1, 0, 2, 3).reshape(group_rows, kv_local * 2 * head_size)
    kv_grads = lax.psum(kv_terms.astype(jnp.bfloat16), "seq")
    local_weight = lax.dot_general(
        traded, kv_grads, (((0,), (0,)), ((), ())), preferred_element_type=jnp.float32
    )
    weight_grad = lax.psum(local_weight * (1.0 / (lax.axis_size("dp") * node_count)), "dp")
    return (attended, query_grad, weight_grad)


def solution(mesh):
    placed = (
        P(("dp", "seq"), "tensor"),
        P(("dp", "seq"), "tensor"),
        P("seq", "tensor"),
        P("dp", None),
        P(("dp", "seq"), "tensor"),
    )
    return jax.shard_map(
        per_device,
        mesh=mesh,
        in_specs=placed,
        out_specs=(P(("dp", "seq"), "tensor"), P(("dp", "seq"), "tensor"), P("seq", "tensor")),
        check_vma=False,
    )
```

profile of v0, /device:TPU:8, one launch (start us, length us, event | category | flops | bytes accessed | tf_op | source)
XLA Modules:
  0.0 414.3 jit_solution(17990220807136559389)
XLA Ops:
  13.4 45.1 %all-gather.2.cloned.1.call-done = bf16[128,8192]{0,1:T(8,128)(2,1)} async-done(((bf16[128,1024]{0,1:T(8,128)(2,1)}), bf16[128,8192]{0,1:T(8,128)(2,1)}) %all-gather.2.cloned.1.call-update) | async-done | bytes 2097168 | tf_op jit(solution)/shard_map/all_gather | solution.py:44
  58.4 7.5 %all-to-all-start = ((bf16[128,16,512]{0,2,1:T(8,128)(2,1)}), bf16[128,16,512]{0,2,1:T(8,128)(2,1)S(1)}, u32[]{:S(2)}, u32[]{:S(2)}) async-start(bf16[128,16,512]{0,2,1:T(8,128)(2,1)} %bitcast.163), calls=%async_computation | async-start | bytes 4194304 | tf_op jit(solution)/shard_map/all_to_all | solution.py:45
  66.0 40.3 %while.42 = (s32[]{:T(128)}, s32[]{:T(128)}, s32[16]{0:T(128)S(1)}, s32[16]{0:T(128)S(1)}, s32[]{:T(128)}, /*index=5*/s32[]{:T(128)}, s32[]{:T(128)}) while((s32[]{:T(128)}, s32[]{:T(128)}, s32[16]{0:T(128)S(1)}, s32[16]{0:T(128)S(1)}, s32[]{:T(128)}, /*index=5*/s32[]{:T(128)}, s32[]{:T(128)}) %tuple.73), condition=%wide.region_2.3_spmd.clone, body=%wide.region_1.2_spmd.clone.sunk | while | flops 70 | bytes 273 | solution.py:58
  106.4 8.8 %all-to-all-done = bf16[128,16,512]{0,2,1:T(8,128)(2,1)S(1)} async-done(((bf16[128,16,512]{0,2,1:T(8,128)(2,1)}), bf16[128,16,512]{0,2,1:T(8,128)(2,1)S(1)}, u32[]{:S(2)}, u32[]{:S(2)}) %all-to-all-start) | async-done | bytes 2097184 | tf_op jit(solution)/shard_map/all_to_all | solution.py:45
  116.5 2.9 copy.38
  119.4 2.0 fusion.48
  121.4 60.2 %all-reduce.7 = bf16[2048,256]{1,0:T(8,128)(2,1)} all-reduce(f32[2048,256]{1,0:T(8,128)} %fusion.48), channel_id=1, replica_groups=mesh['dp'=4,'seq'=16,'tensor'=8] {'seq'}, use_global_device_ids=true, to_apply=%region_0.0 | all-reduce | flops 524288 | bytes 3145728 | tf_op jit(solution)/shard_map/psum | solution.py:47
  181.6 2.2 squeeze.41
  183.8 3.2 fusion.47
  188.9 39.9 %while.43 = (s32[]{:T(128)}, f32[2048,128]{1,0:T(8,128)}, f32[2048,128]{1,0:T(8,128)}, bf16[2,128,4,128]{3,1,2,0:T(8,128)(2,1)}, f32[2,128,4,128]{3,1,2,0:T(8,12...) while((s32[]{:T(128)}, f32[2048,128]{1,0:T(8,128)}, ...), condition=%wide.region_7.8_spmd.clone, body=%wide.region_3.7_spmd.clone.sunk | while | flops 1626342912 | bytes 79985504 | solution.py:88
  189.8 1.9 fusion.91
  191.7 1.9 copy-done.2
  195.4 1.8 multiply_reduce_fusion.2
  197.2 4.5 %fusion.93 = bf16[4,128,2048]{2,1,0:T(8,128)(2,1)} fusion(f32[4,128]{1,0:T(4,128)S(1)} %bitcast.169, f32[4,128,2048]{2,1,0:T(8,128)} %copy-done.2, f32[4,128]{1,0:T(4,128)} %copy-done.11, bf16[2048,128]{0,1:T(8,128)(2,1)} %get-tuple-element.411, bf16[1,128,4,128]{1,3,2,0:T(8,128)(2,1)S(1)} %constant_dynamic-slice_fusion.3), kind=kOutput, calls=%fused_computation.9.clone.1 | convolution fusion | flops 273678336 | bytes 6950912 | tf_op jit(solution)/shard_map/while/body/eval_jaxpr/while/body/eval_jaxpr/thd,jd->htj/dot_general | solution.py:22
  201.8 3.5 fusion.94
  209.7 1.9 fusion.91
  211.6 1.9 copy-done.2
  215.2 1.8 multiply_reduce_fusion.2
  217.1 4.5 %fusion.93 = bf16[4,128,2048]{2,1,0:T(8,128)(2,1)} fusion(f32[4,128]{1,0:T(4,128)S(1)} %bitcast.169, f32[4,128,2048]{2,1,0:T(8,128)} %copy-done.2, f32[4,128]{1,0:T(4,128)} %copy-done.11, bf16[2048,128]{0,1:T(8,128)(2,1)} %get-tuple-element.411, bf16[1,128,4,128]{1,3,2,0:T(8,128)(2,1)S(1)} %constant_dynamic-slice_fusion.3), kind=kOutput, calls=%fused_computation.9.clone.1 | convolution fusion | flops 273678336 | bytes 6950912 | tf_op jit(solution)/shard_map/while/body/eval_jaxpr/while/body/eval_jaxpr/thd,jd->htj/dot_general | solution.py:22
  221.6 3.8 fusion.94
  233.0 116.3 %all-reduce.4.cloned.1.call-done = bf16[2048,256]{0,1:T(8,128)(2,1)} async-done(((bf16[2048,256]{0,1:T(8,128)(2,1)}), bf16[2048,256]{0,1:T(8,128)(2,1)}) %all-reduce.4.cloned.1.call-update) | async-done | bytes 1048592 | tf_op jit(solution)/shard_map/psum | solution.py:95
  349.3 2.7 fusion.37
  355.5 50.2 %all-reduce.6.cloned.1.call-done = f32[512,256]{0,1:T(8,128)} async-done(((f32[512,256]{0,1:T(8,128)}), f32[512,256]{0,1:T(8,128)}) %all-reduce.6.cloned.1.call-update) | async-done | bytes 524304 | tf_op jit(solution)/shard_map/psum | solution.py:99
  405.7 2.0 copy.48
  (114 shorter events, 38.6 us)
Async XLA Ops:
  7.2 112.2 %copy-start = (bf16[512,256]{1,0:T(8,128)(2,1)S(1)}, bf16[512,256]{1,0:T(8,128)(2,1)}, u32[]{:S(2)}) copy-start(bf16[512,256]{1,0:T(8,128)(2,1)} %param.11) | copy-start | bytes 786436
  7.2 58.8 %copy-start.12 = (s32[1,16]{1,0:T(1,128)S(1)}, s32[1,16]{1,0:T(1,128)}, u32[]{:S(2)}) copy-start(s32[1,16]{1,0:T(1,128)} %param.12) | copy-start | bytes 196
  7.2 51.3 %all-gather.2.cloned.1.call-start = ((), (), s32[]{:S(2)}) async-start(), calls=%async_computation.1 | async-start | bytes 2359296 | tf_op jit(solution)/shard_map/all_gather | solution.py:44
  58.4 56.7 %all-to-all-start = ((bf16[128,16,512]{0,2,1:T(8,128)(2,1)}), bf16[128,16,512]{0,2,1:T(8,128)(2,1)S(1)}, u32[]{:S(2)}, u32[]{:S(2)}) async-start(bf16[128,16,512]{0,2,1:T(8,128)(2,1)} %bitcast.163), calls=%async_computation | async-start | bytes 4194304 | tf_op jit(solution)/shard_map/all_to_all | solution.py:45
  65.9 283.4 %all-reduce.4.cloned.1.call-start = ((), (), s32[]{:S(2)}) async-start(), calls=%async_computation.2 | async-start | bytes 2097152 | tf_op jit(solution)/shard_map/psum | solution.py:95
  115.2 1.3 copy-start.7
  119.4 62.2 %copy-start.5 = (bf16[16,128,512]{2,1,0:T(8,128)(2,1)}, bf16[16,128,512]{2,1,0:T(8,128)(2,1)S(1)}, u32[]{:S(2)}) copy-start(bf16[16,128,512]{2,1,0:T(8,128)(2,1)S(1)} %copy.38) | copy-start | bytes 6291460
  191.7 2.0 copy-start.2
  191.7 2.6 copy-start.11
  201.8 3.6 copy-start.1
  201.8 3.6 copy-start.8
  201.8 4.3 %copy-start.3 = (f32[2048,128]{1,0:T(8,128)S(1)}, f32[2048,128]{1,0:T(8,128)}, u32[]{:S(2)}) copy-start(f32[2048,128]{1,0:T(8,128)} %get-tuple-element.391) | copy-start | bytes 3145732 | tf_op jit(solution)/shard_map/while/body/eval_jaxpr/while
  206.0 2.0 copy-start.9
  207.1 1.0 copy-start.4
  211.5 2.0 copy-start.2
  211.5 2.6 copy-start.11
  221.6 3.8 copy-start.1
  221.6 3.8 copy-start.8
  221.6 4.5 %copy-start.3 = (f32[2048,128]{1,0:T(8,128)S(1)}, f32[2048,128]{1,0:T(8,128)}, u32[]{:S(2)}) copy-start(f32[2048,128]{1,0:T(8,128)} %get-tuple-element.391) | copy-start | bytes 3145732 | tf_op jit(solution)/shard_map/while/body/eval_jaxpr/while
  226.1 2.0 copy-start.9
  227.2 1.0 copy-start.4
  228.8 120.5 %copy-start.6 = (bf16[16,128,512]{2,1,0:T(8,128)(2,1)S(1)}, bf16[16,128,512]{2,1,0:T(8,128)(2,1)}, u32[]{:S(2)}) copy-start(bf16[16,128,512]{2,1,0:T(8,128)(2,1)} %copy-done.5) | copy-start | bytes 6291460
  232.9 119.2 %copy-start.10 = (f32[2,128,4,128]{3,1,2,0:T(8,128)S(1)}, f32[2,128,4,128]{3,1,2,0:T(8,128)}, u32[]{:S(2)}) copy-start(f32[2,128,4,128]{3,1,2,0:T(8,128)} %get-tuple-element.111) | copy-start | bytes 1572868
  232.9 172.8 %all-reduce.6.cloned.1.call-start = ((), (), s32[]{:S(2)}) async-start(), calls=%async_computation.3 | async-start | bytes 1048576 | tf_op jit(solution)/shard_map/psum | solution.py:99
Sparse Core Ops, SparseCore 0:
  10.7 47.7 all-gather.1
  233.1 116.2 all-reduce.3
  352.2 53.4 all-reduce.5
where the time goes:
time: 415 us; the launch traced here: 414 us
  waiting for transfers between devices  220 us (53%)
  blocking collectives  60.2 us (15%)
  local copies, waits for them, and re-layouts  44.7 us (11%)
  loops' own time  30.9 us (7%)
  matrix products  29.8 us (7%)
  between operations  13.9 us (3%)
  starting transfers between devices  7.6 us (2%)
  other arithmetic  6.75 us (2%)
    psum x1, waiting for transfers between devices, per_device(): kv_grads = lax.psum(kv_terms.astype(jnp.bfloat16), 'seq')  116 us
    psum x1, blocking collectives, per_device(): kv_all = lax.psum(partial_kv, 'seq').astype(jnp.bfloat16)  60.2 us
    psum x1, waiting for transfers between devices, per_device(): lax.psum(local_weight * (1.0 / (lax.axis_size('dp') * node_count)), 'dp')  50.2 us
    all_gather x1, waiting for transfers between devices, per_device(): whole_rows = lax.all_gather(hidden, 'tensor', axis=1, tiled=True)  45.1 us
    another operation x1, loops' own time, per_device(): final_pair = lax.fori_loop(0, node_count, follow, start_pair)  30.7 us
    unnamed x18, local copies, waits for them, and re-layouts  10 us
    dynamic_slice x16, local copies, waits for them, and re-layouts, follow(): current = jnp.where(current >= 0, parent_list[jnp.maximum(current, 0)], -1)  9.39 us
    dot_general x2, matrix products, attend_block(): jnp.einsum('thd,jd->htj', grad_blk, values_head, preferred_element_type=j...  9.07 us
  transfers between devices with their start and end apart: 4, of which 4 were waited for; matrix products, arithmetic and copies ran while one was open for 4% of the time, Pallas kernels for 0%

commit v1 on v0

--- a/solution.py
+++ b/solution.py
@@ -3,8 +3,16 @@
 import jax.numpy as jnp
 from jax import lax
 from jax.sharding import PartitionSpec as P
+from jax.lax import all_to_all, axis_size
 
 HD = 128
+
+
+def search_copies_in(in_dim, x0):
+    return jnp.concatenate(
+        all_to_all(jnp.stack(tuple((x0 for _ in range(axis_size("tensor"))))), "tensor", 0, 0),
+        axis=in_dim,
+    )
 
 
 def attend_block(query_blk, grad_blk, keys_head, values_head, visible):
@@ -41,7 +49,7 @@
     node_count = lax.axis_size("seq")
     my_node = lax.axis_index("seq")
     group_rows = tok_rows * node_count
-    whole_rows = lax.all_gather(hidden, "tensor", axis=1, tiled=True)
+    whole_rows = search_copies_in(1, hidden)
     traded = lax.all_to_all(whole_rows, "seq", split_axis=1, concat_axis=0, tiled=True)
     partial_kv = jnp.dot(traded, kv_weight, preferred_element_type=jnp.float32)
     kv_all = lax.psum(partial_kv, "seq").astype(jnp.bfloat16)

time: 415 us -> 426 us (1.027)
  starting transfers between devices: 7.6 us -> 20.5 us
    all_to_all x0 -> x1, waiting for transfers between devices: none -> 45.6 us  [search_copies_in(): all_to_all(jnp.stack(tuple((x0 for _ in range(axis_size('tensor'))))), 't...]
    all_gather x1 -> x0, waiting for transfers between devices: 45.1 us -> none  [per_device(): whole_rows = lax.all_gather(hidden, 'tensor', axis=1, tiled=True)]
    all_to_all x0 -> x1, starting transfers between devices: none -> 10 us  [search_copies_in(): all_to_all(jnp.stack(tuple((x0 for _ in range(axis_size('tensor'))))), 't...]
    unnamed x18 -> x22, local copies, waits for them, and re-layouts: 10 us -> 7.48 us
  transfers between devices with their start and end apart: 4 -> 4, of which waited for: 4 -> 4; matrix products, arithmetic and copies ran while one was open for 4% -> 3% of each run, Pallas kernels for 0% -> 0%
where the time goes in v1:
time: 426 us; the launch traced here: 425 us
  waiting for transfers between devices  221 us (52%)
  blocking collectives  60.2 us (14%)
  local copies, waits for them, and re-layouts  42.5 us (10%)
  loops' own time  29.8 us (7%)
  matrix products  29.8 us (7%)
  starting transfers between devices  20.5 us (5%)
  between operations  14.2 us (3%)
  other arithmetic  6.75 us (2%)
    psum x1, waiting for transfers between devices, per_device(): kv_grads = lax.psum(kv_terms.astype(jnp.bfloat16), 'seq')  115 us
    psum x1, blocking collectives, per_device(): kv_all = lax.psum(partial_kv, 'seq').astype(jnp.bfloat16)  60.2 us
    psum x1, waiting for transfers between devices, per_device(): lax.psum(local_weight * (1.0 / (lax.axis_size('dp') * node_count)), 'dp')  50.2 us
    all_to_all x1, waiting for transfers between devices, search_copies_in(): all_to_all(jnp.stack(tuple((x0 for _ in range(axis_size('tensor'))))), 't...  45.6 us
    another operation x1, loops' own time, per_device(): final_pair = lax.fori_loop(0, node_count, follow, start_pair)  29.6 us
    all_to_all x1, starting transfers between devices, per_device(): lax.all_to_all(whole_rows, 'seq', split_axis=1, concat_axis=0, tiled=True)  10.4 us
    all_to_all x1, waiting for transfers between devices, per_device(): lax.all_to_all(whole_rows, 'seq', split_axis=1, concat_axis=0, tiled=True)  10.4 us
    all_to_all x1, starting transfers between devices, search_copies_in(): all_to_all(jnp.stack(tuple((x0 for _ in range(axis_size('tensor'))))), 't...  10 us
  transfers between devices with their start and end apart: 4, of which 4 were waited for; matrix products, arithmetic and copies ran while one was open for 3% of the time, Pallas kernels for 0%

profile of v1, /device:TPU:8, one launch (start us, length us, event | category | flops | bytes accessed | tf_op | source)
XLA Modules:
  0.0 425.0 jit_solution(10208193679815595699)
XLA Ops:
  10.0 10.0 %all-to-all-start = ((bf16[8,128,1024]{1,2,0:T(8,128)(2,1)}), bf16[8,128,1024]{1,2,0:T(8,128)(2,1)}, u32[]{:S(2)}, u32[]{:S(2)}) async-start(bf16[8,128,1024]{1,2,0:T(8,128)(2,1)} %stack.26), calls=%async_computation | async-start | bytes 4194304 | tf_op jit(solution)/shard_map/all_to_all | solution.py:13
  21.8 45.6 %all-to-all-done = bf16[8,128,1024]{1,2,0:T(8,128)(2,1)} async-done(((bf16[8,128,1024]{1,2,0:T(8,128)(2,1)}), bf16[8,128,1024]{1,2,0:T(8,128)(2,1)}, u32[]{:S(2)}, u32[]{:S(2)}) %all-to-all-start) | async-done | bytes 2097184 | tf_op jit(solution)/shard_map/all_to_all | solution.py:13
  67.4 10.4 %all-to-all-start.1 = ((bf16[128,16,512]{0,2,1:T(8,128)(2,1)}), bf16[128,16,512]{0,2,1:T(8,128)(2,1)S(1)}, u32[]{:S(2)}, u32[]{:S(2)}) async-start(bf16[128,16,512]{0,2,1:T(8,128)(2,1)} %bitcast.4), calls=%async_computation.1 | async-start | bytes 4194304 | tf_op jit(solution)/shard_map/all_to_all | solution.py:53
  77.9 38.7 %while.42 = (s32[]{:T(128)}, s32[]{:T(128)}, s32[16]{0:T(128)S(1)}, s32[16]{0:T(128)S(1)}, s32[]{:T(128)}, /*index=5*/s32[]{:T(128)}, s32[]{:T(128)}) while((s32[]{:T(128)}, s32[]{:T(128)}, s32[16]{0:T(128)S(1)}, s32[16]{0:T(128)S(1)}, s32[]{:T(128)}, /*index=5*/s32[]{:T(128)}, s32[]{:T(128)}) %tuple.69), condition=%wide.region_2.3_spmd.clone, body=%wide.region_1.2_spmd.clone.sunk | while | flops 70 | bytes 273 | solution.py:66
  116.7 10.4 %all-to-all-done.1 = bf16[128,16,512]{0,2,1:T(8,128)(2,1)S(1)} async-done(((bf16[128,16,512]{0,2,1:T(8,128)(2,1)}), bf16[128,16,512]{0,2,1:T(8,128)(2,1)S(1)}, u32[]{:S(2)}, u32[]{:S(2)}) %all-to-all-start.1) | async-done | bytes 2097184 | tf_op jit(solution)/shard_map/all_to_all | solution.py:53
  128.4 2.9 copy.23
  131.3 2.0 fusion.48
  133.3 60.2 %all-reduce.7 = bf16[2048,256]{1,0:T(8,128)(2,1)} all-reduce(f32[2048,256]{1,0:T(8,128)} %fusion.48), channel_id=1, replica_groups=mesh['dp'=4,'seq'=16,'tensor'=8] {'seq'}, use_global_device_ids=true, to_apply=%region_0.0 | all-reduce | flops 524288 | bytes 3145728 | tf_op jit(solution)/shard_map/psum | solution.py:55
  193.5 2.2 squeeze.41
  195.6 3.2 fusion.47
  200.7 39.9 %while.43 = (s32[]{:T(128)}, f32[2048,128]{1,0:T(8,128)}, f32[2048,128]{1,0:T(8,128)}, bf16[2,128,4,128]{3,1,2,0:T(8,128)(2,1)}, f32[2,128,4,128]{3,1,2,0:T(8,12...) while((s32[]{:T(128)}, f32[2048,128]{1,0:T(8,128)}, ...), condition=%wide.region_7.8_spmd.clone, body=%wide.region_3.7_spmd.clone.sunk | while | flops 1626342912 | bytes 79985504 | solution.py:96
  201.7 1.9 fusion.91
  203.5 1.9 copy-done.2
  207.2 1.8 multiply_reduce_fusion.2
  209.0 4.5 %fusion.93 = bf16[4,128,2048]{2,1,0:T(8,128)(2,1)} fusion(f32[4,128]{1,0:T(4,128)S(1)} %bitcast.170, f32[4,128,2048]{2,1,0:T(8,128)} %copy-done.2, f32[4,128]{1,0:T(4,128)} %copy-done.13, bf16[2048,128]{0,1:T(8,128)(2,1)} %get-tuple-element.396, bf16[1,128,4,128]{1,3,2,0:T(8,128)(2,1)S(1)} %constant_dynamic-slice_fusion.3), kind=kOutput, calls=%fused_computation.9.clone.1 | convolution fusion | flops 273678336 | bytes 6950912 | tf_op jit(solution)/shard_map/while/body/eval_jaxpr/while/body/eval_jaxpr/thd,jd->htj/dot_general | solution.py:30
  213.6 3.5 fusion.94
  221.5 1.9 fusion.91
  223.4 1.9 copy-done.2
  228.9 4.5 %fusion.93 = bf16[4,128,2048]{2,1,0:T(8,128)(2,1)} fusion(f32[4,128]{1,0:T(4,128)S(1)} %bitcast.170, f32[4,128,2048]{2,1,0:T(8,128)} %copy-done.2, f32[4,128]{1,0:T(4,128)} %copy-done.13, bf16[2048,128]{0,1:T(8,128)(2,1)} %get-tuple-element.396, bf16[1,128,4,128]{1,3,2,0:T(8,128)(2,1)S(1)} %constant_dynamic-slice_fusion.3), kind=kOutput, calls=%fused_computation.9.clone.1 | convolution fusion | flops 273678336 | bytes 6950912 | tf_op jit(solution)/shard_map/while/body/eval_jaxpr/while/body/eval_jaxpr/thd,jd->htj/dot_general | solution.py:30
  233.4 3.8 fusion.94
  244.8 114.9 %all-reduce.4.cloned.1.call-done = bf16[2048,256]{0,1:T(8,128)(2,1)} async-done(((bf16[2048,256]{0,1:T(8,128)(2,1)}), bf16[2048,256]{0,1:T(8,128)(2,1)}) %all-reduce.4.cloned.1.call-update) | async-done | bytes 1048592 | tf_op jit(solution)/shard_map/psum | solution.py:103
  359.7 2.7 fusion.37
  365.8 50.2 %all-reduce.6.cloned.1.call-done = f32[512,256]{0,1:T(8,128)} async-done(((f32[512,256]{0,1:T(8,128)}), f32[512,256]{0,1:T(8,128)}) %all-reduce.6.cloned.1.call-update) | async-done | bytes 524304 | tf_op jit(solution)/shard_map/psum | solution.py:107
  416.1 2.0 copy.33
  (118 shorter events, 38.4 us)
Async XLA Ops:
  7.2 124.1 %copy-start = (bf16[512,256]{1,0:T(8,128)(2,1)S(1)}, bf16[512,256]{1,0:T(8,128)(2,1)}, u32[]{:S(2)}) copy-start(bf16[512,256]{1,0:T(8,128)(2,1)} %param.11) | copy-start | bytes 786436
  7.2 12.8 %copy-start.11 = (bf16[128,1024]{1,0:T(8,128)(2,1)S(1)}, bf16[128,1024]{1,0:T(8,128)(2,1)}, u32[]{:S(2)}) copy-start(bf16[128,1024]{1,0:T(8,128)(2,1)} %param.13) | copy-start | bytes 786436
  7.2 13.7 %copy-start.12 = (bf16[128,1024]{1,0:T(8,128)(2,1)S(1)}, bf16[128,1024]{1,0:T(8,128)(2,1)}, u32[]{:S(2)}) copy-start(bf16[128,1024]{1,0:T(8,128)(2,1)} %param.10) | copy-start | bytes 786436
  7.2 13.9 %copy-start.14 = (s32[1,16]{1,0:T(1,128)S(1)}, s32[1,16]{1,0:T(1,128)}, u32[]{:S(2)}) copy-start(s32[1,16]{1,0:T(1,128)} %param.12) | copy-start | bytes 196
  10.0 57.4 %all-to-all-start = ((bf16[8,128,1024]{1,2,0:T(8,128)(2,1)}), bf16[8,128,1024]{1,2,0:T(8,128)(2,1)}, u32[]{:S(2)}, u32[]{:S(2)}) async-start(bf16[8,128,1024]{1,2,0:T(8,128)(2,1)} %stack.26), calls=%async_computation | async-start | bytes 4194304 | tf_op jit(solution)/shard_map/all_to_all | solution.py:13
  67.4 59.7 %all-to-all-start.1 = ((bf16[128,16,512]{0,2,1:T(8,128)(2,1)}), bf16[128,16,512]{0,2,1:T(8,128)(2,1)S(1)}, u32[]{:S(2)}, u32[]{:S(2)}) async-start(bf16[128,16,512]{0,2,1:T(8,128)(2,1)} %bitcast.4), calls=%async_computation.1 | async-start | bytes 4194304 | tf_op jit(solution)/shard_map/all_to_all | solution.py:53
  77.8 281.9 %all-reduce.4.cloned.1.call-start = ((), (), s32[]{:S(2)}) async-start(), calls=%async_computation.2 | async-start | bytes 2097152 | tf_op jit(solution)/shard_map/psum | solution.py:103
  127.0 1.3 copy-start.7
  131.2 62.2 %copy-start.5 = (bf16[16,128,512]{2,1,0:T(8,128)(2,1)}, bf16[16,128,512]{2,1,0:T(8,128)(2,1)S(1)}, u32[]{:S(2)}) copy-start(bf16[16,128,512]{2,1,0:T(8,128)(2,1)S(1)} %copy.23) | copy-start | bytes 6291460
  203.5 2.0 copy-start.2
  203.5 2.6 copy-start.13
  213.6 3.6 copy-start.1
  213.6 3.6 copy-start.8
  213.6 4.3 %copy-start.3 = (f32[2048,128]{1,0:T(8,128)S(1)}, f32[2048,128]{1,0:T(8,128)}, u32[]{:S(2)}) copy-start(f32[2048,128]{1,0:T(8,128)} %get-tuple-element.376) | copy-start | bytes 3145732 | tf_op jit(solution)/shard_map/while/body/eval_jaxpr/while
  217.8 2.0 copy-start.9
  223.3 2.0 copy-start.2
  223.3 2.6 copy-start.13
  233.4 3.8 copy-start.1
  233.4 3.8 copy-start.8
  233.4 4.5 %copy-start.3 = (f32[2048,128]{1,0:T(8,128)S(1)}, f32[2048,128]{1,0:T(8,128)}, u32[]{:S(2)}) copy-start(f32[2048,128]{1,0:T(8,128)} %get-tuple-element.376) | copy-start | bytes 3145732 | tf_op jit(solution)/shard_map/while/body/eval_jaxpr/while
  237.9 2.0 copy-start.9
  240.6 119.1 %copy-start.6 = (bf16[16,128,512]{2,1,0:T(8,128)(2,1)S(1)}, bf16[16,128,512]{2,1,0:T(8,128)(2,1)}, u32[]{:S(2)}) copy-start(bf16[16,128,512]{2,1,0:T(8,128)(2,1)} %copy-done.5) | copy-start | bytes 6291460
  244.7 117.7 %copy-start.10 = (f32[2,128,4,128]{3,1,2,0:T(8,128)S(1)}, f32[2,128,4,128]{3,1,2,0:T(8,128)}, u32[]{:S(2)}) copy-start(f32[2,128,4,128]{3,1,2,0:T(8,128)} %get-tuple-element.111) | copy-start | bytes 1572868
  244.8 171.3 %all-reduce.6.cloned.1.call-start = ((), (), s32[]{:S(2)}) async-start(), calls=%async_computation.3 | async-start | bytes 1048576 | tf_op jit(solution)/shard_map/psum | solution.py:107
  (2 other events, 1.9 us)
Sparse Core Ops, SparseCore 0:
  244.9 114.7 all-reduce.3
  362.6 53.4 all-reduce.5
